TPU v7x, 32 devices: a whole 2x2x4 slice. The times are simulated.
32 devices in a mesh: dp: 8 (over z, y), mp: 4 (over x, core).
Axes of the slice: x: 2, y: 2, z: 4, core: 2. Of those that a mesh axis runs over, the one named last changes fastest.
Arguments:
- token_ids: int32 [16384], P('dp'), may hold values from 0 to 8191
- seg_ids: int32 [16384], P('dp'), may hold values from 0 to 255, as said below
- timesteps: int32 [16384], P('dp'), may hold values from 0 to 1999
- noise: float32 [16384, 128], P('dp'), may hold values from -6 to 6
- table: bfloat16 [8192, 128], P('dp'), may hold values from -6 to 6
- w_in: bfloat16 [128, 768], replicated, may hold values from -0.5 to 0.5
- b_in: float32 [768], replicated, may hold values from -3 to 3
- w_time: bfloat16 [128, 768], replicated, may hold values from -0.5 to 0.5
- gain1: float32 [768], replicated, may hold values from 0.5 to 1.5
- shift1: float32 [768], replicated, may hold values from -2 to 2
- w_qkv: bfloat16 [3, 768, 768], P(None, None, 'mp'), may hold values from -0.21875 to 0.21875
- w_out: bfloat16 [768, 768], P('mp'), may hold values from -3.5 to 3.5
- gain2: float32 [768], replicated, may hold values from 0.5 to 1.5
- shift2: float32 [768], replicated, may hold values from -2 to 2
- w_up: bfloat16 [768, 3072], P(None, 'mp'), may hold values from -0.21875 to 0.21875
- b_up: float32 [3072], P('mp'), may hold values from -2 to 2
- w_down: bfloat16 [3072, 768], P('mp'), may hold values from -0.109375 to 0.109375
- b_down: float32 [768], replicated, may hold values from -2 to 2
- cotangent: float32 [16384, 768], P('dp'), may hold values from -6 to 6
Outputs:
- output: float32 [16384, 768], P('dp')
- grad_table: float32 [8192, 128], P('dp')
- grad_w_in: float32 [128, 768], replicated
- grad_b_in: float32 [768], replicated
- grad_w_time: float32 [128, 768], replicated
- grad_gain1: float32 [768], replicated
- grad_shift1: float32 [768], replicated
- grad_w_qkv: float32 [3, 768, 768], P(None, None, 'mp')
- grad_w_out: float32 [768, 768], P('mp')
- grad_gain2: float32 [768], replicated
- grad_shift2: float32 [768], replicated
- grad_w_up: float32 [768, 3072], P(None, 'mp')
- grad_b_up: float32 [3072], P('mp')
- grad_w_down: float32 [3072, 768], P('mp')
- grad_b_down: float32 [768], replicated
Inputs may be any that keep to these rules, and one draw needn't show every extreme that they name: `seg_ids`: slots fall into aligned runs of 1024; each run is either one document or 16 documents of 64 slots; ids never fall along the slots and differ between runs; the first run is one document and the last is split.
All inputs are finite; a program needn't handle non-finite values.
Results may differ from a plain program's by a relative error of at most 0.017.
Values may be sent and summed in bfloat16 or wider, within the bound.
No kernel may reach another device: no remote copies, remote signals or barrier semaphores. Data moves between devices by JAX's collectives and lax.ppermute only.
A program may use at most 192 MiB of HBM per device.

v0:
```python
import math
import jax
import jax.numpy as jnp
from jax import lax
from jax.sharding import PartitionSpec as P

HD = 64
TSTEPS = 2000
QBLK = 512
NEG_BIG = -1000000000.0


def layer_norm(inputs, gain_vec, shift_vec):
    row_mean = jnp.mean(inputs, axis=-1, keepdims=True)
    centred = inputs - row_mean
    variance = jnp.mean(centred * centred, axis=-1, keepdims=True)
    return centred * lax.rsqrt(variance + 1e-05) * gain_vec + shift_vec


def noise_rates(time_ids, horizon):
    fraction = time_ids.astype(jnp.float32) / horizon
    signal = 1.0 - jnp.sqrt(fraction + 0.0001)
    return (jnp.sqrt(signal), jnp.sqrt(1.0 - signal))


def time_features(time_ids, feat_width):
    half_width = feat_width // 2
    freq_table = jnp.exp(
        -math.log(10000.0) * jnp.arange(half_width, dtype=jnp.float32) / half_width
    )
    angles = time_ids.astype(jnp.float32)[:, None] * freq_table[None, :]
    return jnp.concatenate([jnp.sin(angles), jnp.cos(angles)], axis=1)


def gelu_exact(inputs):
    return jax.nn.gelu(inputs, approximate=False)


def block_rows(array_in, index, block_len):
    return lax.dynamic_slice_in_dim(array_in, index * block_len, block_len, 0)


def masked_scores(query_blk, key_blk, seg_query, seg_key):
    scaled = jnp.einsum(
        "qhd,khd->hqk", query_blk, key_blk, preferred_element_type=jnp.float32
    ) * query_blk.shape[-1] ** (-0.5)
    same_seg = seg_query[:, None] == seg_key[None, :]
    return jnp.where(same_seg[None], scaled, NEG_BIG)


def attend_forward(queries, keys_all, values_all, seg_ids, block_len):
    token_count, head_count, head_width = queries.shape
    block_count = token_count // block_len

    def query_block(q_index):
        query_blk = block_rows(queries, q_index, block_len)
        seg_query = block_rows(seg_ids, q_index, block_len)

        def stats_step(k_index, current):
            row_top, row_sum = current
            scores = masked_scores(
                query_blk,
                block_rows(keys_all, k_index, block_len),
                seg_query,
                block_rows(seg_ids, k_index, block_len),
            )
            new_top = jnp.maximum(row_top, jnp.max(scores, axis=-1))
            new_sum = row_sum * jnp.exp(row_top - new_top) + jnp.sum(
                jnp.exp(scores - new_top[:, :, None]), axis=-1
            )
            return (new_top, new_sum)

        start_stats = (
            jnp.full((head_count, block_len), NEG_BIG, jnp.float32),
            jnp.zeros((head_count, block_len), jnp.float32),
        )
        row_top, row_sum = lax.fori_loop(0, block_count, stats_step, start_stats)

        def value_step(k_index, current):
            scores = masked_scores(
                query_blk,
                block_rows(keys_all, k_index, block_len),
                seg_query,
                block_rows(seg_ids, k_index, block_len),
            )
            weights_bf = (jnp.exp(scores - row_top[:, :, None]) / row_sum[:, :, None]).astype(
                jnp.bfloat16
            )
            return current + jnp.einsum(
                "hqk,khd->qhd",
                weights_bf,
                block_rows(values_all, k_index, block_len),
                preferred_element_type=jnp.float32,
            )

        mixed_blk = lax.fori_loop(
            0, block_count, value_step, jnp.zeros((block_len, head_count, head_width), jnp.float32)
        )
        return (mixed_blk, row_top, row_sum)

    mixed_all, tops, sums = lax.map(query_block, jnp.arange(block_count))
    return (mixed_all.reshape(token_count, head_count, head_width), tops, sums)


def attend_backward(queries, keys_all, values_all, grad_mixed, seg_ids, tops, sums, block_len):
    token_count, head_count, head_width = queries.shape
    block_count = token_count // block_len
    scale_factor = head_width ** (-0.5)

    def query_step(q_index, totals):
        grad_q_all, grad_k_all, grad_v_all = totals
        query_blk = block_rows(queries, q_index, block_len)
        grad_blk = block_rows(grad_mixed, q_index, block_len)
        seg_query = block_rows(seg_ids, q_index, block_len)
        row_top = tops[q_index]
        row_sum = sums[q_index]

        def probs_for(k_index):
            key_blk = block_rows(keys_all, k_index, block_len)
            value_blk = block_rows(values_all, k_index, block_len)
            scores = masked_scores(
                query_blk, key_blk, seg_query, block_rows(seg_ids, k_index, block_len)
            )
            weights = jnp.exp(scores - row_top[:, :, None]) / row_sum[:, :, None]
            grad_weights = jnp.einsum(
                "qhd,khd->hqk", grad_blk, value_blk, preferred_element_type=jnp.float32
            )
            return (key_blk, weights, grad_weights)

        def delta_step(k_index, current):
            key_blk, weights, grad_weights = probs_for(k_index)
            return current + jnp.sum(grad_weights * weights, axis=-1)

        delta = lax.fori_loop(
            0, block_count, delta_step, jnp.zeros((head_count, block_len), jnp.float32)
        )

        def grad_step(k_index, current):
            grad_query, grad_keys, grad_values = current
            key_blk, weights, grad_weights = probs_for(k_index)
            grad_scores = (weights * (grad_weights - delta[:, :, None])).astype(jnp.bfloat16)
            grad_query = (
                grad_query
                + jnp.einsum(
                    "hqk,khd->qhd", grad_scores, key_blk, preferred_element_type=jnp.float32
                )
                * scale_factor
            )
            key_part = (
                jnp.einsum(
                    "hqk,qhd->khd", grad_scores, query_blk, preferred_element_type=jnp.float32
                )
                * scale_factor
            )
            value_part = jnp.einsum(
                "hqk,qhd->khd",
                weights.astype(jnp.bfloat16),
                grad_blk,
                preferred_element_type=jnp.float32,
            )
            grad_keys = lax.dynamic_update_slice_in_dim(
                grad_keys,
                block_rows(grad_keys, k_index, block_len) + key_part,
                k_index * block_len,
                0,
            )
            grad_values = lax.dynamic_update_slice_in_dim(
                grad_values,
                block_rows(grad_values, k_index, block_len) + value_part,
                k_index * block_len,
                0,
            )
            return (grad_query, grad_keys, grad_values)

        start_grads = (
            jnp.zeros((block_len, head_count, head_width), jnp.float32),
            grad_k_all,
            grad_v_all,
        )
        grad_query, grad_k_all, grad_v_all = lax.fori_loop(0, block_count, grad_step, start_grads)
        grad_q_all = lax.dynamic_update_slice_in_dim(grad_q_all, grad_query, q_index * block_len, 0)
        return (grad_q_all, grad_k_all, grad_v_all)

    zeros_all = jnp.zeros(queries.shape, jnp.float32)
    return lax.fori_loop(0, block_count, query_step, (zeros_all, zeros_all, zeros_all))


def body(
    token_ids,
    seg_ids,
    timesteps,
    noise,
    table,
    w_in,
    b_in,
    w_time,
    gain1,
    shift1,
    w_qkv,
    w_out,
    gain2,
    shift2,
    w_up,
    b_up,
    w_down,
    b_down,
    cotangent,
):
    whole_table = lax.all_gather(table, "dp", axis=0, tiled=True)
    table_full = whole_table.astype(jnp.float32)
    vocab_rows, embed_width = table_full.shape
    row_norms = jnp.sqrt(jnp.sum(table_full * table_full, axis=1) + 1e-06)
    mean_norm = jnp.mean(row_norms)
    factor = math.sqrt(embed_width) / mean_norm
    looked_up = jnp.take(table_full, token_ids, axis=0)
    clean_rows = looked_up * factor
    keep_rate, noise_rate = noise_rates(timesteps, TSTEPS)
    noisy_in = (keep_rate[:, None] * clean_rows + noise_rate[:, None] * noise).astype(jnp.bfloat16)
    features = time_features(timesteps, w_time.shape[0]).astype(jnp.bfloat16)
    hidden = (
        jnp.dot(noisy_in, w_in, preferred_element_type=jnp.float32)
        + jnp.dot(features, w_time, preferred_element_type=jnp.float32)
        + b_in
    )
    token_count = hidden.shape[0]
    act_one_f, norm_one_back = jax.vjp(layer_norm, hidden, gain1, shift1)
    act_one = act_one_f.astype(jnp.bfloat16)
    projected = jnp.einsum(
        "td,cdk->ctk", act_one, w_qkv, preferred_element_type=jnp.float32
    ).astype(jnp.bfloat16)
    head_count = w_qkv.shape[2] // HD
    heads_all = projected.reshape(3, token_count, head_count, HD)
    queries, keys_all, values_all = (heads_all[0], heads_all[1], heads_all[2])
    mixed_f, tops, sums = attend_forward(queries, keys_all, values_all, seg_ids, QBLK)
    mixed = mixed_f.astype(jnp.bfloat16).reshape(token_count, head_count * HD)
    attn_part = jnp.dot(mixed, w_out, preferred_element_type=jnp.float32)
    resid = hidden + lax.psum(attn_part, "mp")
    act_two_f, norm_two_back = jax.vjp(layer_norm, resid, gain2, shift2)
    act_two = act_two_f.astype(jnp.bfloat16)
    pre_act = jnp.dot(act_two, w_up, preferred_element_type=jnp.float32) + b_up
    activated_f, gelu_back = jax.vjp(gelu_exact, pre_act)
    activated = activated_f.astype(jnp.bfloat16)
    down_part = jnp.dot(activated, w_down, preferred_element_type=jnp.float32)
    output = resid + lax.psum(down_part.astype(jnp.bfloat16), "mp").astype(jnp.float32) + b_down
    cot_rounded = cotangent.astype(jnp.bfloat16)
    grad_w_down = jnp.einsum(
        "tf,td->fd", activated, cot_rounded, preferred_element_type=jnp.float32
    )
    grad_b_down = jnp.sum(cotangent, axis=0)
    grad_gelu = jnp.einsum("td,fd->tf", cot_rounded, w_down, preferred_element_type=jnp.float32)
    (grad_pre,) = gelu_back(grad_gelu)
    grad_pre_r = grad_pre.astype(jnp.bfloat16)
    grad_w_up = jnp.einsum("td,tf->df", act_two, grad_pre_r, preferred_element_type=jnp.float32)
    grad_b_up = jnp.sum(grad_pre_r.astype(jnp.float32), axis=0)
    grad_two_part = jnp.einsum("tf,df->td", grad_pre_r, w_up, preferred_element_type=jnp.float32)
    grad_act_two = lax.psum(grad_two_part, "mp")
    grad_resid_norm, grad_gain2, grad_shift2 = norm_two_back(grad_act_two)
    grad_resid = cotangent + grad_resid_norm
    grad_attn_r = grad_resid.astype(jnp.bfloat16)
    grad_w_out = jnp.einsum("tk,td->kd", mixed, grad_attn_r, preferred_element_type=jnp.float32)
    grad_mixed = (
        jnp.einsum("td,kd->tk", grad_attn_r, w_out, preferred_element_type=jnp.float32)
        .astype(jnp.bfloat16)
        .reshape(token_count, head_count, HD)
    )
    grad_q, grad_k, grad_v = attend_backward(
        queries, keys_all, values_all, grad_mixed, seg_ids, tops, sums, QBLK
    )
    grad_proj = jnp.stack(
        [grad_q.astype(jnp.bfloat16), grad_k.astype(jnp.bfloat16), grad_v.astype(jnp.bfloat16)]
    ).reshape(3, token_count, head_count * HD)
    grad_w_qkv = jnp.einsum("td,ctk->cdk", act_one, grad_proj, preferred_element_type=jnp.float32)
    grad_one_part = jnp.einsum("ctk,cdk->td", grad_proj, w_qkv, preferred_element_type=jnp.float32)
    grad_act_one = lax.psum(grad_one_part.astype(jnp.bfloat16), "mp").astype(jnp.float32)
    grad_hidden_norm, grad_gain1, grad_shift1 = norm_one_back(grad_act_one)
    grad_hidden_r = (grad_resid + grad_hidden_norm).astype(jnp.bfloat16)
    grad_w_in = jnp.einsum("te,td->ed", noisy_in, grad_hidden_r, preferred_element_type=jnp.float32)
    grad_w_time = jnp.einsum(
        "te,td->ed", features, grad_hidden_r, preferred_element_type=jnp.float32
    )
    grad_b_in = jnp.sum(grad_hidden_r.astype(jnp.float32), axis=0)
    grad_noisy = jnp.einsum("td,ed->te", grad_hidden_r, w_in, preferred_element_type=jnp.float32)
    grad_clean = keep_rate[:, None] * grad_noisy
    scaled_grad = grad_clean * factor
    norm_coeff = -jnp.sum(grad_clean * looked_up) * factor / (mean_norm * vocab_rows)
    unit_rows = table_full / row_norms[:, None]
    row_count = lax.axis_size("dp") * table.shape[0]
    inside = (token_ids >= 0) & (token_ids < row_count)
    slot_ids = jnp.where(inside, token_ids, row_count)
    direct = jax.ops.segment_sum(scaled_grad, slot_ids, num_segments=row_count + 1)[:row_count]
    grad_table = lax.psum_scatter(
        direct + norm_coeff * unit_rows, "dp", scatter_dimension=0, tiled=True
    )
    summed = tuple(
        lax.psum(
            (
                grad_w_in,
                grad_b_in,
                grad_w_time,
                grad_gain1,
                grad_shift1,
                grad_w_qkv,
                grad_w_out,
                grad_gain2,
                grad_shift2,
                grad_w_up,
                grad_b_up,
                grad_w_down,
                grad_b_down,
            ),
            "dp",
        )
    )
    return (
        output,
        grad_table,
        summed[0],
        summed[1],
        summed[2],
        summed[3],
        summed[4],
        summed[5],
        summed[6],
        summed[7],
        summed[8],
        summed[9],
        summed[10],
        summed[11],
        summed[12],
    )


def solution(mesh):
    in_specs = (
        P("dp"),
        P("dp"),
        P("dp"),
        P("dp", None),
        P("dp", None),
        P(),
        P(),
        P(),
        P(),
        P(),
        P(None, None, "mp"),
        P("mp", None),
        P(),
        P(),
        P(None, "mp"),
        P("mp"),
        P("mp", None),
        P(),
        P("dp", None),
    )
    out_specs = (
        P("dp", None),
        P("dp", None),
        P(),
        P(),
        P(),
        P(),
        P(),
        P(None, None, "mp"),
        P("mp", None),
        P(),
        P(),
        P(None, "mp"),
        P("mp"),
        P("mp", None),
        P(),
    )
    return jax.shard_map(body, mesh=mesh, in_specs=in_specs, out_specs=out_specs, check_vma=False)
```

profile of v0, /device:TPU:0, one launch (start us, length us, event | category | flops | bytes accessed | tf_op | source)
XLA Modules:
  0.0 1170.5 jit_solution(15731865098663500380)
XLA Ops:
  13.5 48.5 %all-gather.2.cloned.1.call-done = bf16[8192,128]{1,0:T(8,128)(2,1)} async-done(((bf16[1024,128]{1,0:T(8,128)(2,1)}), bf16[8192,128]{1,0:T(8,128)(2,1)}) %all-gather.2.cloned.1.call-update) | async-done | bytes 2097168 | tf_op jit(solution)/shard_map/all_gather | solution.py:209
  66.6 3.9 convert_element_type.97
  70.5 7.7 gather_fusion
  78.2 3.3 add_convert_fusion.4
  90.6 98.2 %while.123 = (s32[]{:T(128)}, bf16[4,512,3,64]{1,3,2,0:T(8,128)(2,1)}, f32[4,3,512]{2,1,0:T(4,128)}, f32[4,3,512]{2,1,0:T(4,128)}, s32[4]{0:T(128)S(1)}, /*index...) while((s32[]{:T(128)}, ...), condition=%wide.region_11.12_spmd, body=%wide.region_4.11_spmd.sunk | while | flops 312155648 | bytes 10699101 | solution.py:101
  92.8 7.4 while.127
  100.9 12.5 %while.128 = (s32[]{:T(128)}, f32[512,3,64]{0,2,1:T(8,128)}, bf16[2048,3,64]{0,2,1:T(8,128)(2,1)S(1)}, s32[512]{0:T(512)S(1)}, s32[2048]{0:T(1024)S(1)}, /*index...) while((s32[]{:T(128)}, f32[512,3,64]{0,2,1:T(8,128)}, ...), condition=%wide.region_10.10_spmd.clone, body=%wide.region_9.9_spmd.clone.sunk | while | flops 205717504 | bytes 1926848 | solution.py:96
  117.3 7.4 while.127
  125.4 12.5 %while.128 = (s32[]{:T(128)}, f32[512,3,64]{0,2,1:T(8,128)}, bf16[2048,3,64]{0,2,1:T(8,128)(2,1)S(1)}, s32[512]{0:T(512)S(1)}, s32[2048]{0:T(1024)S(1)}, /*index...) while((s32[]{:T(128)}, f32[512,3,64]{0,2,1:T(8,128)}, ...), condition=%wide.region_10.10_spmd.clone, body=%wide.region_9.9_spmd.clone.sunk | while | flops 205717504 | bytes 1926848 | solution.py:96
  141.8 7.4 while.127
  149.8 12.5 %while.128 = (s32[]{:T(128)}, f32[512,3,64]{0,2,1:T(8,128)}, bf16[2048,3,64]{0,2,1:T(8,128)(2,1)S(1)}, s32[512]{0:T(512)S(1)}, s32[2048]{0:T(1024)S(1)}, /*index...) while((s32[]{:T(128)}, f32[512,3,64]{0,2,1:T(8,128)}, ...), condition=%wide.region_10.10_spmd.clone, body=%wide.region_9.9_spmd.clone.sunk | while | flops 205717504 | bytes 1926848 | solution.py:96
  166.3 7.4 while.127
  174.3 12.5 %while.128 = (s32[]{:T(128)}, f32[512,3,64]{0,2,1:T(8,128)}, bf16[2048,3,64]{0,2,1:T(8,128)(2,1)S(1)}, s32[512]{0:T(512)S(1)}, s32[2048]{0:T(1024)S(1)}, /*index...) while((s32[]{:T(128)}, f32[512,3,64]{0,2,1:T(8,128)}, ...), condition=%wide.region_10.10_spmd.clone, body=%wide.region_9.9_spmd.clone.sunk | while | flops 205717504 | bytes 1926848 | solution.py:96
  191.9 3.7 fusion.100
  195.6 118.2 %all-reduce.8.cloned.1.call-done = f32[2048,768]{0,1:T(8,128)} async-done(((f32[2048,768]{0,1:T(8,128)}), f32[2048,768]{0,1:T(8,128)}) %all-reduce.8.cloned.1.call-update) | async-done | bytes 6291472 | tf_op jit(solution)/shard_map/psum | solution.py:237
  313.9 6.2 fusion.96
  323.0 18.8 %multiply_convert_fusion = (bf16[2048,768]{1,0:T(8,128)(2,1)}, f32[2048,768]{1,0:T(8,128)}, f32[2048,768]{1,0:T(8,128)}) fusion(f32[768]{0:T(1024)S(1)} %copy-done.63, bf16[2048,768]{0,1:T(8,128)(2,1)S(1)} %add_convert_fusion.2, bf16[768,768]{1,0:T(8,128)(2,1)S(1)} %copy-done), kind=kOutput, calls=%fused_computation.93 | convolution fusion | flops 2519728128 | bytes 20057088 | tf_op jit(solution)/shard_map/dot_general | solution.py:240
  341.8 8.1 convert_reduce_fusion.1
  351.6 4.5 fusion.101
  356.1 7.0 copy.74
  364.1 6.0 convolution_convert_fusion
  370.1 105.9 %all-reduce.10.cloned.1.call-done = f32[2048,768]{0,1:T(8,128)} async-done(((f32[2048,768]{0,1:T(8,128)}), f32[2048,768]{0,1:T(8,128)}) %all-reduce.10.cloned.1.call-update) | async-done | bytes 6291472 | tf_op jit(solution)/shard_map/psum | solution.py:256
  476.1 6.5 multiply_reduce_fusion
  482.6 4.0 fusion.94
  492.9 161.6 %while.126 = (s32[]{:T(128)}, bf16[2048,3,64]{0,2,1:T(8,128)(2,1)}, f32[2048,3,64]{0,2,1:T(8,128)}, f32[2048,3,64]{0,2,1:T(8,128)S(1)}, bf16[2048,3,64]{0,2,1:T(...) while((s32[]{:T(128)}, bf16[2048,3,64]{0,2,1:T(8,128)(2,1)}, ...), condition=%wide.region_25.26_spmd, body=%wide.region_19.25_spmd.sunk | while | flops 716768768 | bytes 27696096 | solution.py:185
  494.7 12.6 %while.129 = (s32[]{:T(128)}, f32[3,512]{1,0:T(4,128)S(1)}, bf16[2048,3,64]{0,2,1:T(8,128)(2,1)}, bf16[512,3,64]{0,2,1:T(8,128)(2,1)S(1)}, s32[512]{0:T(512)S(1)...) while((s32[]{:T(128)}, f32[3,512]{1,0:T(4,128)S(1)}, ...), condition=%wide.region_22.22_spmd.clone, body=%wide.region_20.21_spmd.clone.sunk | while | flops 206308864 | bytes 7647441 | solution.py:134
  507.3 25.2 %while.130 = (s32[]{:T(128)}, f32[512,3,64]{0,2,1:T(8,128)S(1)}, f32[2048,3,64]{0,2,1:T(8,128)}, f32[2048,3,64]{0,2,1:T(8,128)S(1)}, bf16[2048,3,64]{0,2,1:T(8,1...) while((s32[]{:T(128)}, f32[512,3,64]{0,2,1:T(8,128)S(1)}, ...), condition=%wide.region_24.24_spmd.clone, body=%wide.region_23.23_spmd.clone.sunk | while | flops 510459904 | bytes 18446580 | solution.py:180
  535.1 12.6 %while.129 = (s32[]{:T(128)}, f32[3,512]{1,0:T(4,128)S(1)}, bf16[2048,3,64]{0,2,1:T(8,128)(2,1)}, bf16[512,3,64]{0,2,1:T(8,128)(2,1)S(1)}, s32[512]{0:T(512)S(1)...) while((s32[]{:T(128)}, f32[3,512]{1,0:T(4,128)S(1)}, ...), condition=%wide.region_22.22_spmd.clone, body=%wide.region_20.21_spmd.clone.sunk | while | flops 206308864 | bytes 7647441 | solution.py:134
  547.7 25.2 %while.130 = (s32[]{:T(128)}, f32[512,3,64]{0,2,1:T(8,128)S(1)}, f32[2048,3,64]{0,2,1:T(8,128)}, f32[2048,3,64]{0,2,1:T(8,128)S(1)}, bf16[2048,3,64]{0,2,1:T(8,1...) while((s32[]{:T(128)}, f32[512,3,64]{0,2,1:T(8,128)S(1)}, ...), condition=%wide.region_24.24_spmd.clone, body=%wide.region_23.23_spmd.clone.sunk | while | flops 510459904 | bytes 18446580 | solution.py:180
  575.5 12.6 %while.129 = (s32[]{:T(128)}, f32[3,512]{1,0:T(4,128)S(1)}, bf16[2048,3,64]{0,2,1:T(8,128)(2,1)}, bf16[512,3,64]{0,2,1:T(8,128)(2,1)S(1)}, s32[512]{0:T(512)S(1)...) while((s32[]{:T(128)}, f32[3,512]{1,0:T(4,128)S(1)}, ...), condition=%wide.region_22.22_spmd.clone, body=%wide.region_20.21_spmd.clone.sunk | while | flops 206308864 | bytes 7647441 | solution.py:134
  588.1 25.2 %while.130 = (s32[]{:T(128)}, f32[512,3,64]{0,2,1:T(8,128)S(1)}, f32[2048,3,64]{0,2,1:T(8,128)}, f32[2048,3,64]{0,2,1:T(8,128)S(1)}, bf16[2048,3,64]{0,2,1:T(8,1...) while((s32[]{:T(128)}, f32[512,3,64]{0,2,1:T(8,128)S(1)}, ...), condition=%wide.region_24.24_spmd.clone, body=%wide.region_23.23_spmd.clone.sunk | while | flops 510459904 | bytes 18446580 | solution.py:180
  615.9 12.6 %while.129 = (s32[]{:T(128)}, f32[3,512]{1,0:T(4,128)S(1)}, bf16[2048,3,64]{0,2,1:T(8,128)(2,1)}, bf16[512,3,64]{0,2,1:T(8,128)(2,1)S(1)}, s32[512]{0:T(512)S(1)...) while((s32[]{:T(128)}, f32[3,512]{1,0:T(4,128)S(1)}, ...), condition=%wide.region_22.22_spmd.clone, body=%wide.region_20.21_spmd.clone.sunk | while | flops 206308864 | bytes 7647441 | solution.py:134
  628.4 25.2 %while.130 = (s32[]{:T(128)}, f32[512,3,64]{0,2,1:T(8,128)S(1)}, f32[2048,3,64]{0,2,1:T(8,128)}, f32[2048,3,64]{0,2,1:T(8,128)S(1)}, bf16[2048,3,64]{0,2,1:T(8,1...) while((s32[]{:T(128)}, f32[512,3,64]{0,2,1:T(8,128)S(1)}, ...), condition=%wide.region_24.24_spmd.clone, body=%wide.region_23.23_spmd.clone.sunk | while | flops 510459904 | bytes 18446580 | solution.py:180
  657.3 5.8 bitcast_convert_fusion
  663.2 7.0 fusion.104
  670.3 7.1 fusion.70
  682.7 100.5 %all-reduce.14.cloned.1.call-done = (bf16[2048,768]{0,1:T(8,128)(2,1)}, bf16[2048,768]{0,1:T(8,128)(2,1)}) async-done(((bf16[2048,768]{0,1:T(8,128)(2,1)}, bf16[2048,768]{0,1:T(8,128)(2,1)}), (bf16[2048,768]{0,1:T(8,128)(2,1)}, bf16[2048,768]{0,1:T(8,128)(2,1)})) %all-reduce.14.cloned.1.call-update) | async-done | bytes 6291472 | tf_op jit(solution)/shard_map/psum | solution.py:244
  783.1 5.7 convert_reduce_fusion
  788.9 5.7 fusion.59
  794.7 5.8 convert_reduce_fusion.2
  804.6 5.0 multiply_reduce_fusion.5
  811.0 13.1 %scatter_custom_fusion = f32[8193,128]{1,0:T(8,128)} fusion(s32[2048]{0:T(1024)} %get-tuple-element.1347, f32[]{:T(128)} %constant.325.clone.1, f32[2048,128]{1,0:T(8,128)} %get-tuple-element.1355, f32[]{:T(128)S(6)} %div.136), kind=kCustom, calls=%fused_computation.122 | custom fusion | flops 524288 | bytes 5243908 | tf_op jit(solution)/shard_map/scatter-add | solution.py:290
  824.1 6.6 slice_add_fusion
  834.0 7.1 add_add_fusion.3
  841.2 6.6 copy.77
  847.8 40.1 %all-reduce = (f32[768]{0:T(1024)}, f32[768]{0:T(1024)}, f32[768]{0:T(1024)}, f32[768]{0:T(1024)}, f32[768]{0:T(1024)}, /*index=5*/f32[768]{0:T(1024)}, f32[768]{0:T(1024)}) all-reduce(f32[768]{0:T(1024)S(1)} %get-tuple-element.1324, f32[768]{0:T(1024)S(1)} %get-tuple-element.1186, ...), channel_id=1, replica_groups=mesh['dp'=8,'mp'=4] {'dp'}, use_global_device_ids=true, to_apply=%region_34.35 | all-reduce | flops 5376 | bytes 43008 | tf_op jit(solution)/shard_map/psum | solution.py:295
  887.9 172.8 %all-reduce.12.cloned.1.call-done = (f32[128,768]{1,0:T(8,128)}, f32[128,768]{1,0:T(8,128)}, f32[3,768,192]{1,2,0:T(8,128)}, f32[192,768]{1,0:T(8,128)}, f32[768,768]{1,0:T(8,128)}, /*index=5*/f32[768,768]{1,0:T(8,128)}) async-done(((f32[128,768]{1,0:T(8,128)}, f32[128,768]{1,0:T(8,128)}, f32[3,768,192]{1,2,0:T(8,128)}, f32[192,768]{1,0:T(8,128)}, f32[768,768]{1,0:T(8,128)}, ...) | async-done | bytes 7864336 | tf_op jit(solution)/shard_map/psum | solution.py:295
  1060.6 91.4 %reduce-scatter.2.cloned.1.call-done = f32[1024,128]{1,0:T(8,128)} async-done(((f32[8192,128]{1,0:T(8,128)}), f32[1024,128]{1,0:T(8,128)}) %reduce-scatter.2.cloned.1.call-update) | async-done | bytes 524304 | tf_op jit(solution)/shard_map/reduce_scatter | solution.py:291
  (619 shorter events, 315.0 us)
Async XLA Ops:
  7.2 315.8 %copy-start = (bf16[768,768]{1,0:T(8,128)(2,1)S(1)}, bf16[768,768]{1,0:T(8,128)(2,1)}, u32[]{:S(2)}) copy-start(bf16[768,768]{1,0:T(8,128)(2,1)} %param.45) | copy-start | bytes 3538948
  7.2 54.8 %all-gather.2.cloned.1.call-start = ((), (), s32[]{:S(2)}) async-start(), calls=%async_computation.1 | async-start | bytes 2359296 | tf_op jit(solution)/shard_map/all_gather | solution.py:209
  7.9 305.9 %all-reduce.8.cloned.1.call-start = ((), (), s32[]{:S(2)}) async-start(), calls=%async_computation.2 | async-start | bytes 12582912 | tf_op jit(solution)/shard_map/psum | solution.py:237
  9.4 68.8 %copy-start.51 = (pred[2048]{0:T(1024)(128)(4,1)}, pred[2048]{0:T(1024)(128)(4,1)S(1)}, u32[]{:S(2)}) copy-start(pred[2048]{0:T(1024)(128)(4,1)S(1)} %compare_and_fusion) | copy-start | bytes 6148
  11.4 66.8 %copy-start.39 = (f32[2048]{0:T(1024)}, f32[2048]{0:T(1024)S(1)}, u32[]{:S(2)}) copy-start(f32[2048]{0:T(1024)S(1)} %get-tuple-element.1349) | copy-start | bytes 24580
  13.5 69.2 %copy-start.23 = (bf16[2048,64]{0,1:T(8,128)(2,1)}, bf16[2048,64]{0,1:T(8,128)(2,1)S(1)}, u32[]{:S(2)}) copy-start(bf16[2048,64]{0,1:T(8,128)(2,1)S(1)} %get-tuple-element.1345) | copy-start | bytes 786436
  13.5 69.2 %copy-start.25 = (bf16[2048,64]{0,1:T(8,128)(2,1)}, bf16[2048,64]{0,1:T(8,128)(2,1)S(1)}, u32[]{:S(2)}) copy-start(bf16[2048,64]{0,1:T(8,128)(2,1)S(1)} %get-tuple-element.1346) | copy-start | bytes 786436
  70.5 11.1 copy-start.35
  90.5 101.3 %copy-start.29 = (bf16[192,768]{1,0:T(8,128)(2,1)S(1)}, bf16[192,768]{1,0:T(8,128)(2,1)}, u32[]{:S(2)}) copy-start(bf16[192,768]{1,0:T(8,128)(2,1)} %param.42) | copy-start | bytes 884740
  188.7 6.8 copy-start.6
  195.6 280.5 %all-reduce.10.cloned.1.call-start = ((), (), s32[]{:S(2)}) async-start(), calls=%async_computation.3 | async-start | bytes 12582912 | tf_op jit(solution)/shard_map/psum | solution.py:256
  320.8 20.9 %slice-start.2 = ((s8[6291456]{0:T(1024)(128)(4,1)}), s8[4194304]{0:T(1024)(128)(4,1)S(1)}, s32[]{:S(2)}) async-start(s8[6291456]{0:T(1024)(128)(4,1)} %bitcast.204), calls=%async_computation.9 | async-start | bytes 8388608
  322.9 18.8 %copy-start.21 = (bf16[2048,768]{0,1:T(8,128)(2,1)}, bf16[2048,768]{0,1:T(8,128)(2,1)S(1)}, u32[]{:S(2)}) copy-start(bf16[2048,768]{0,1:T(8,128)(2,1)S(1)} %add_convert_fusion.2) | copy-start | bytes 9437188
  322.9 18.8 %slice-start.3 = ((s8[6291456]{0:T(1024)(128)(4,1)}), s8[2097152]{0:T(1024)(128)(4,1)S(1)}, s32[]{:S(2)}) async-start(s8[6291456]{0:T(1024)(128)(4,1)} %bitcast.204), calls=%async_computation.10 | async-start | bytes 4194304
  322.9 18.8 %copy-start.61 = (bf16[768,768]{1,0:T(8,128)(2,1)S(1)}, bf16[768,768]{1,0:T(8,128)(2,1)}, u32[]{:S(2)}) copy-start(bf16[768,768]{1,0:T(8,128)(2,1)} %param.47) | copy-start | bytes 3538948
  356.1 427.0 %all-reduce.14.cloned.1.call-start = ((), (), s32[]{:S(2)}) async-start(), calls=%async_computation.6 | async-start | bytes 12582912 | tf_op jit(solution)/shard_map/psum | solution.py:244
  476.0 6.5 copy-start.10
  476.0 10.6 slice-start.4
  654.6 8.5 copy-start.31
  663.2 397.5 %all-reduce.12.cloned.1.call-start = ((), (), s32[]{:S(2)}) async-start(), calls=%async_computation.5 | async-start | bytes 15728640 | tf_op jit(solution)/shard_map/psum | solution.py:295
  663.2 7.0 copy-start.22
  670.2 7.1 copy-start.8
  670.2 7.1 copy-start.15
  670.2 9.1 copy-start.20
  670.2 9.1 copy-start.30
  670.2 9.1 copy-start.32
  670.2 9.1 copy-start.34
  679.4 103.8 %copy-start.38 = (f32[2048]{0:T(1024)S(1)}, f32[2048]{0:T(1024)}, u32[]{:S(2)}) copy-start(f32[2048]{0:T(1024)} %copy-done.37) | copy-start | bytes 24580
  679.4 103.7 %copy-start.50 = (f32[768]{0:T(1024)S(1)}, f32[768]{0:T(1024)}, u32[]{:S(2)}) copy-start(f32[768]{0:T(1024)} %param.39) | copy-start | bytes 9220
  679.4 115.2 %slice-start.6 = ((s8[6291456]{0:T(1024)(128)(4,1)}), s8[2097152]{0:T(1024)(128)(4,1)S(1)}, s32[]{:S(2)}) async-start(s8[6291456]{0:T(1024)(128)(4,1)} %bitcast.208), calls=%async_computation.13 | async-start | bytes 4194304
  682.7 106.2 %copy-start.48 = (f32[2048]{0:T(1024)S(1)}, f32[2048]{0:T(1024)}, u32[]{:S(2)}) copy-start(f32[2048]{0:T(1024)} %copy-done.47) | copy-start | bytes 24580
  682.7 106.3 %copy-start.44 = (f32[2048]{0:T(1024)S(1)}, f32[2048]{0:T(1024)}, u32[]{:S(2)}) copy-start(f32[2048]{0:T(1024)} %copy-done.43) | copy-start | bytes 24580
  783.1 5.8 copy-start.9
  783.1 11.5 slice-start
  783.1 11.5 slice-start.7
  788.9 5.8 copy-start.46
  794.7 5.8 copy-start.24
  794.7 5.8 copy-start.26
  794.7 7.8 copy-start.17
  804.5 19.6 %copy-start.11 = (bf16[8192,128]{1,0:T(8,128)(2,1)S(1)}, bf16[8192,128]{1,0:T(8,128)(2,1)}, u32[]{:S(2)}) copy-start(bf16[8192,128]{1,0:T(8,128)(2,1)} %all-gather.2.cloned.1.call-done) | copy-start | bytes 6291460
  804.5 19.6 %copy-start.42 = (f32[8192]{0:T(1024)S(1)}, f32[8192]{0:T(1024)}, u32[]{:S(2)}) copy-start(f32[8192]{0:T(1024)} %get-tuple-element.1343) | copy-start | bytes 98308
  804.5 347.5 %reduce-scatter.2.cloned.1.call-start = ((), (), s32[]{:S(2)}) async-start(), calls=%async_computation.4 | async-start | bytes 4718592 | tf_op jit(solution)/shard_map/reduce_scatter | solution.py:291
  841.1 6.6 copy-start.54
  841.1 6.6 copy-start.55
  841.1 6.6 copy-start.60
  1060.6 101.3 %copy-start.27 = (f32[768,768]{1,0:T(8,128)S(1)}, f32[768,768]{1,0:T(8,128)}, u32[]{:S(2)}) copy-start(f32[768,768]{1,0:T(8,128)} %get-tuple-element.2138) | copy-start | bytes 7077892
  1152.0 8.5 copy-start.28
  1153.9 9.4 copy-start.1
  (31 other events, 67.4 us)
Sparse Core Ops, SparseCore 0:
  10.1 51.7 all-gather.1
  195.7 118.1 all-reduce.7
  356.2 119.7 all-reduce.9
  663.3 119.7 all-reduce.13
  804.6 256.0 all-reduce.11
  1064.7 87.2 reduce-scatter.1
where the time goes:
time: 1180 us; the launch traced here: 1170 us
  waiting for transfers between devices  638 us (54%)
  matrix products  279 us (24%)
  other arithmetic  115 us (10%)
  local copies, waits for them, and re-layouts  75.5 us (6%)
  blocking collectives  40.1 us (3%)
  between operations  17.5 us (1%)
    psum x1, waiting for transfers between devices, body(): lax.psum((grad_w_in, grad_b_in, grad_w_time, grad_gain1, grad_shift1, gra...  173 us
    psum x1, waiting for transfers between devices, body(): resid = hidden + lax.psum(attn_part, 'mp')  118 us
    psum x1, waiting for transfers between devices, body(): grad_act_two = lax.psum(grad_two_part, 'mp')  106 us
    psum x1, waiting for transfers between devices, body(): lax.psum(down_part.astype(jnp.bfloat16), 'mp').astype(jnp.float32)  100 us
    reduce_scatter x1, waiting for transfers between devices, body(): lax.psum_scatter(direct + norm_coeff * unit_rows, 'dp', scatter_dimension...  91.4 us
    dot_general x32, matrix products, probs_for(): jnp.einsum('qhd,khd->hqk', grad_blk, value_blk, preferred_element_type=jn...  59.4 us
    all_gather x1, waiting for transfers between devices, body(): whole_table = lax.all_gather(table, 'dp', axis=0, tiled=True)  48.5 us
    dot_general x16, matrix products, value_step(): jnp.einsum('hqk,khd->qhd', weights_bf, block_rows(values_all, k_index, bl...  45.2 us
  transfers between devices with their start and end apart: 6, of which 6 were waited for; matrix products, arithmetic and copies ran while one was open for 7% of the time, Pallas kernels for 0%

commit v1 on v0

--- a/solution.py
+++ b/solution.py
@@ -206,6 +206,11 @@
     b_down,
     cotangent,
 ):
+
+    def screen_handle(a0, shard_axis):
+        reply = lax.all_gather(a0, shard_axis).sum(axis=0)
+        return reply
+
     whole_table = lax.all_gather(table, "dp", axis=0, tiled=True)
     table_full = whole_table.astype(jnp.float32)
     vocab_rows, embed_width = table_full.shape
@@ -253,7 +258,7 @@
     grad_w_up = jnp.einsum("td,tf->df", act_two, grad_pre_r, preferred_element_type=jnp.float32)
     grad_b_up = jnp.sum(grad_pre_r.astype(jnp.float32), axis=0)
     grad_two_part = jnp.einsum("tf,df->td", grad_pre_r, w_up, preferred_element_type=jnp.float32)
-    grad_act_two = lax.psum(grad_two_part, "mp")
+    grad_act_two = screen_handle(grad_two_part, "mp")
     grad_resid_norm, grad_gain2, grad_shift2 = norm_two_back(grad_act_two)
     grad_resid = cotangent + grad_resid_norm
     grad_attn_r = grad_resid.astype(jnp.bfloat16)

time: 1180 us -> 1240 us (1.051)
  other arithmetic: 115 us -> 140 us
  waiting for transfers between devices: 638 us -> 660 us
    all_gather x0 -> x1, waiting for transfers between devices: none -> 140 us  [screen_handle(): reply = lax.all_gather(a0, shard_axis).sum(axis=0)]
    psum x1 -> x0, waiting for transfers between devices: 106 us -> none  [body(): grad_act_two = lax.psum(grad_two_part, 'mp')]
    reduce_sum x0 -> x1, other arithmetic: none -> 12.6 us  [screen_handle(): reply = lax.all_gather(a0, shard_axis).sum(axis=0)]
    reduce_sum x3 -> x4, other arithmetic: 17.9 us -> 29.6 us  [layer_norm(): return centred * lax.rsqrt(variance + 1e-05) * gain_vec + shift_vec]
    unnamed x155 -> x153, local copies, waits for them, and re-layouts: 32.4 us -> 32.9 us
  transfers between devices with their start and end apart: 6 -> 6, of which waited for: 6 -> 6; matrix products, arithmetic and copies ran while one was open for 7% -> 8% of each run, Pallas kernels for 0% -> 0%
where the time goes in v1:
time: 1240 us; the launch traced here: 1220 us
  waiting for transfers between devices  660 us (53%)
  matrix products  280 us (23%)
  other arithmetic  140 us (11%)
  local copies, waits for them, and re-layouts  82.7 us (7%)
  blocking collectives  39.4 us (3%)
  between operations  17.6 us (1%)
    psum x1, waiting for transfers between devices, body(): lax.psum((grad_w_in, grad_b_in, grad_w_time, grad_gain1, grad_shift1, gra...  161 us
    all_gather x1, waiting for transfers between devices, screen_handle(): reply = lax.all_gather(a0, shard_axis).sum(axis=0)  140 us
    psum x1, waiting for transfers between devices, body(): resid = hidden + lax.psum(attn_part, 'mp')  118 us
    psum x1, waiting for transfers between devices, body(): lax.psum(down_part.astype(jnp.bfloat16), 'mp').astype(jnp.float32)  100 us
    reduce_scatter x1, waiting for transfers between devices, body(): lax.psum_scatter(direct + norm_coeff * unit_rows, 'dp', scatter_dimension...  91.4 us
    dot_general x32, matrix products, probs_for(): jnp.einsum('qhd,khd->hqk', grad_blk, value_blk, preferred_element_type=jn...  59.4 us
    all_gather x1, waiting for transfers between devices, body(): whole_table = lax.all_gather(table, 'dp', axis=0, tiled=True)  48.5 us
    dot_general x16, matrix products, value_step(): jnp.einsum('hqk,khd->qhd', weights_bf, block_rows(values_all, k_index, bl...  45.2 us
  transfers between devices with their start and end apart: 6, of which 6 were waited for; matrix products, arithmetic and copies ran while one was open for 8% of the time, Pallas kernels for 0%

profile of v1, /device:TPU:0, one launch (start us, length us, event | category | flops | bytes accessed | tf_op | source)
XLA Modules:
  0.0 1225.0 jit_solution(9801567382336779501)
XLA Ops:
  13.5 48.5 %all-gather.4.cloned.1.call-done = bf16[8192,128]{1,0:T(8,128)(2,1)} async-done(((bf16[1024,128]{1,0:T(8,128)(2,1)}), bf16[8192,128]{1,0:T(8,128)(2,1)}) %all-gather.4.cloned.1.call-update) | async-done | bytes 2097168 | tf_op jit(solution)/shard_map/all_gather | solution.py:214
  70.5 7.7 gather_fusion
  90.6 98.2 %while.123 = (s32[]{:T(128)}, bf16[4,512,3,64]{1,3,2,0:T(8,128)(2,1)}, f32[4,3,512]{2,1,0:T(4,128)}, f32[4,3,512]{2,1,0:T(4,128)}, s32[4]{0:T(128)S(1)}, /*index...) while((s32[]{:T(128)}, ...), condition=%wide.region_11.12_spmd, body=%wide.region_4.11_spmd.sunk | while | flops 312155648 | bytes 10699101 | solution.py:101
  92.8 7.4 while.127
  100.9 12.5 %while.128 = (s32[]{:T(128)}, f32[512,3,64]{0,2,1:T(8,128)}, bf16[2048,3,64]{0,2,1:T(8,128)(2,1)S(1)}, s32[512]{0:T(512)S(1)}, s32[2048]{0:T(1024)S(1)}, /*index...) while((s32[]{:T(128)}, f32[512,3,64]{0,2,1:T(8,128)}, ...), condition=%wide.region_10.10_spmd.clone, body=%wide.region_9.9_spmd.clone.sunk | while | flops 205717504 | bytes 1926848 | solution.py:96
  117.3 7.4 while.127
  125.4 12.5 %while.128 = (s32[]{:T(128)}, f32[512,3,64]{0,2,1:T(8,128)}, bf16[2048,3,64]{0,2,1:T(8,128)(2,1)S(1)}, s32[512]{0:T(512)S(1)}, s32[2048]{0:T(1024)S(1)}, /*index...) while((s32[]{:T(128)}, f32[512,3,64]{0,2,1:T(8,128)}, ...), condition=%wide.region_10.10_spmd.clone, body=%wide.region_9.9_spmd.clone.sunk | while | flops 205717504 | bytes 1926848 | solution.py:96
  141.8 7.4 while.127
  149.9 12.5 %while.128 = (s32[]{:T(128)}, f32[512,3,64]{0,2,1:T(8,128)}, bf16[2048,3,64]{0,2,1:T(8,128)(2,1)S(1)}, s32[512]{0:T(512)S(1)}, s32[2048]{0:T(1024)S(1)}, /*index...) while((s32[]{:T(128)}, f32[512,3,64]{0,2,1:T(8,128)}, ...), condition=%wide.region_10.10_spmd.clone, body=%wide.region_9.9_spmd.clone.sunk | while | flops 205717504 | bytes 1926848 | solution.py:96
  166.3 7.4 while.127
  174.4 12.5 %while.128 = (s32[]{:T(128)}, f32[512,3,64]{0,2,1:T(8,128)}, bf16[2048,3,64]{0,2,1:T(8,128)(2,1)S(1)}, s32[512]{0:T(512)S(1)}, s32[2048]{0:T(1024)S(1)}, /*index...) while((s32[]{:T(128)}, f32[512,3,64]{0,2,1:T(8,128)}, ...), condition=%wide.region_10.10_spmd.clone, body=%wide.region_9.9_spmd.clone.sunk | while | flops 205717504 | bytes 1926848 | solution.py:96
  195.7 118.2 %all-reduce.7.cloned.1.call-done = f32[2048,768]{0,1:T(8,128)} async-done(((f32[2048,768]{0,1:T(8,128)}), f32[2048,768]{0,1:T(8,128)}) %all-reduce.7.cloned.1.call-update) | async-done | bytes 6291472 | tf_op jit(solution)/shard_map/psum | solution.py:242
  313.9 6.2 fusion.96
  323.0 18.8 %multiply_convert_fusion = (bf16[2048,768]{1,0:T(8,128)(2,1)}, f32[2048,768]{1,0:T(8,128)}, f32[2048,768]{1,0:T(8,128)}) fusion(f32[768]{0:T(1024)S(1)} %copy-done.62, bf16[2048,768]{0,1:T(8,128)(2,1)S(1)} %add_convert_fusion.2, bf16[768,768]{1,0:T(8,128)(2,1)S(1)} %copy-done), kind=kOutput, calls=%fused_computation.93 | convolution fusion | flops 2519728128 | bytes 20057088 | tf_op jit(solution)/shard_map/dot_general | solution.py:245
  341.8 8.1 convert_reduce_fusion.1
  351.5 4.6 fusion.101
  356.2 7.1 copy.86
  364.2 6.9 convolution_convert_fusion
  371.1 140.2 %all-gather.6.cloned.1.call-done = f32[8192,768]{1,0:T(8,128)} async-done(((f32[2048,768]{1,0:T(8,128)}), f32[8192,768]{1,0:T(8,128)}) %all-gather.6.cloned.1.call-update) | async-done | bytes 25165840 | tf_op jit(solution)/shard_map/all_gather | solution.py:211
  511.3 12.6 %reduce_sum.235 = f32[2048,768]{1,0:T(8,128)} reduce(f32[4,2048,768]{2,1,0:T(8,128)} %bitcast.205, f32[]{:T(128)} %constant.325.clone.1), dimensions={0}, to_apply=%region_16.17 | reduce | flops 4718592 | bytes 31457284 | tf_op jit(solution)/shard_map/reduce_sum | solution.py:211
  523.9 6.7 copy.85
  530.6 6.4 multiply_reduce_fusion
  537.0 4.1 fusion.94
  547.4 161.6 %while.126 = (s32[]{:T(128)}, bf16[2048,3,64]{0,2,1:T(8,128)(2,1)}, f32[2048,3,64]{0,2,1:T(8,128)}, f32[2048,3,64]{0,2,1:T(8,128)S(1)}, bf16[2048,3,64]{0,2,1:T(...) while((s32[]{:T(128)}, bf16[2048,3,64]{0,2,1:T(8,128)(2,1)}, ...), condition=%wide.region_25.26_spmd, body=%wide.region_19.25_spmd.sunk | while | flops 716768768 | bytes 27696096 | solution.py:185
  549.4 12.6 %while.129 = (s32[]{:T(128)}, f32[3,512]{1,0:T(4,128)S(1)}, bf16[2048,3,64]{0,2,1:T(8,128)(2,1)}, bf16[512,3,64]{0,2,1:T(8,128)(2,1)S(1)}, s32[512]{0:T(512)S(1)...) while((s32[]{:T(128)}, f32[3,512]{1,0:T(4,128)S(1)}, ...), condition=%wide.region_22.22_spmd.clone, body=%wide.region_20.21_spmd.clone.sunk | while | flops 206308864 | bytes 7647441 | solution.py:134
  562.0 25.2 %while.130 = (s32[]{:T(128)}, f32[512,3,64]{0,2,1:T(8,128)S(1)}, f32[2048,3,64]{0,2,1:T(8,128)}, f32[2048,3,64]{0,2,1:T(8,128)S(1)}, bf16[2048,3,64]{0,2,1:T(8,1...) while((s32[]{:T(128)}, f32[512,3,64]{0,2,1:T(8,128)S(1)}, ...), condition=%wide.region_24.24_spmd.clone, body=%wide.region_23.23_spmd.clone.sunk | while | flops 510459904 | bytes 18446580 | solution.py:180
  589.7 12.6 %while.129 = (s32[]{:T(128)}, f32[3,512]{1,0:T(4,128)S(1)}, bf16[2048,3,64]{0,2,1:T(8,128)(2,1)}, bf16[512,3,64]{0,2,1:T(8,128)(2,1)S(1)}, s32[512]{0:T(512)S(1)...) while((s32[]{:T(128)}, f32[3,512]{1,0:T(4,128)S(1)}, ...), condition=%wide.region_22.22_spmd.clone, body=%wide.region_20.21_spmd.clone.sunk | while | flops 206308864 | bytes 7647441 | solution.py:134
  602.3 25.2 %while.130 = (s32[]{:T(128)}, f32[512,3,64]{0,2,1:T(8,128)S(1)}, f32[2048,3,64]{0,2,1:T(8,128)}, f32[2048,3,64]{0,2,1:T(8,128)S(1)}, bf16[2048,3,64]{0,2,1:T(8,1...) while((s32[]{:T(128)}, f32[512,3,64]{0,2,1:T(8,128)S(1)}, ...), condition=%wide.region_24.24_spmd.clone, body=%wide.region_23.23_spmd.clone.sunk | while | flops 510459904 | bytes 18446580 | solution.py:180
  630.1 12.6 %while.129 = (s32[]{:T(128)}, f32[3,512]{1,0:T(4,128)S(1)}, bf16[2048,3,64]{0,2,1:T(8,128)(2,1)}, bf16[512,3,64]{0,2,1:T(8,128)(2,1)S(1)}, s32[512]{0:T(512)S(1)...) while((s32[]{:T(128)}, f32[3,512]{1,0:T(4,128)S(1)}, ...), condition=%wide.region_22.22_spmd.clone, body=%wide.region_20.21_spmd.clone.sunk | while | flops 206308864 | bytes 7647441 | solution.py:134
  642.7 25.2 %while.130 = (s32[]{:T(128)}, f32[512,3,64]{0,2,1:T(8,128)S(1)}, f32[2048,3,64]{0,2,1:T(8,128)}, f32[2048,3,64]{0,2,1:T(8,128)S(1)}, bf16[2048,3,64]{0,2,1:T(8,1...) while((s32[]{:T(128)}, f32[512,3,64]{0,2,1:T(8,128)S(1)}, ...), condition=%wide.region_24.24_spmd.clone, body=%wide.region_23.23_spmd.clone.sunk | while | flops 510459904 | bytes 18446580 | solution.py:180
  670.5 12.6 %while.129 = (s32[]{:T(128)}, f32[3,512]{1,0:T(4,128)S(1)}, bf16[2048,3,64]{0,2,1:T(8,128)(2,1)}, bf16[512,3,64]{0,2,1:T(8,128)(2,1)S(1)}, s32[512]{0:T(512)S(1)...) while((s32[]{:T(128)}, f32[3,512]{1,0:T(4,128)S(1)}, ...), condition=%wide.region_22.22_spmd.clone, body=%wide.region_20.21_spmd.clone.sunk | while | flops 206308864 | bytes 7647441 | solution.py:134
  683.0 25.2 %while.130 = (s32[]{:T(128)}, f32[512,3,64]{0,2,1:T(8,128)S(1)}, f32[2048,3,64]{0,2,1:T(8,128)}, f32[2048,3,64]{0,2,1:T(8,128)S(1)}, bf16[2048,3,64]{0,2,1:T(8,1...) while((s32[]{:T(128)}, f32[512,3,64]{0,2,1:T(8,128)S(1)}, ...), condition=%wide.region_24.24_spmd.clone, body=%wide.region_23.23_spmd.clone.sunk | while | flops 510459904 | bytes 18446580 | solution.py:180
  711.8 5.8 bitcast_convert_fusion
  717.9 7.0 fusion.104
  724.9 7.1 fusion.70
  737.3 100.1 %all-reduce.11.cloned.1.call-done = (bf16[2048,768]{0,1:T(8,128)(2,1)}, bf16[2048,768]{0,1:T(8,128)(2,1)}) async-done(((bf16[2048,768]{0,1:T(8,128)(2,1)}, bf16[2048,768]{0,1:T(8,128)(2,1)}), (bf16[2048,768]{0,1:T(8,128)(2,1)}, bf16[2048,768]{0,1:T(8,128)(2,1)})) %all-reduce.11.cloned.1.call-update) | async-done | bytes 6291472 | tf_op jit(solution)/shard_map/psum | solution.py:249
  837.4 5.7 convert_reduce_fusion
  843.2 5.7 fusion.59
  849.0 5.8 convert_reduce_fusion.2
  858.9 5.1 multiply_reduce_fusion.5
  865.3 13.1 %scatter_custom_fusion = f32[8193,128]{1,0:T(8,128)} fusion(s32[2048]{0:T(1024)} %get-tuple-element.1361, f32[]{:T(128)} %constant.325.clone.1, f32[2048,128]{1,0:T(8,128)} %get-tuple-element.1369, f32[]{:T(128)S(6)} %div.136), kind=kCustom, calls=%fused_computation.122 | custom fusion | flops 524288 | bytes 5243908 | tf_op jit(solution)/shard_map/scatter-add | solution.py:295
  878.4 6.9 slice_add_fusion
  888.7 11.8 reduce_sum.245
  900.4 7.3 add_add_fusion.3
  907.8 7.0 copy.90
  914.8 39.4 %all-reduce = (f32[768]{0:T(1024)}, f32[768]{0:T(1024)}, f32[768]{0:T(1024)}, f32[768]{0:T(1024)}, f32[768]{0:T(1024)}, /*index=5*/f32[768]{0:T(1024)}, f32[768]{0:T(1024)}) all-reduce(f32[768]{0:T(1024)S(1)} %get-tuple-element.1338, f32[768]{0:T(1024)S(1)} %get-tuple-element.1201, ...), channel_id=1, replica_groups=mesh['dp'=8,'mp'=4] {'dp'}, use_global_device_ids=true, to_apply=%region_34.35 | all-reduce | flops 5376 | bytes 43008 | tf_op jit(solution)/shard_map/psum | solution.py:300
  954.2 160.7 %all-reduce.9.cloned.1.call-done = (f32[128,768]{1,0:T(8,128)}, f32[128,768]{1,0:T(8,128)}, f32[3,768,192]{1,2,0:T(8,128)}, f32[192,768]{1,0:T(8,128)}, f32[768,768]{1,0:T(8,128)}, /*index=5*/f32[768,768]{1,0:T(8,128)}) async-done(((f32[128,768]{1,0:T(8,128)}, f32[128,768]{1,0:T(8,128)}, f32[3,768,192]{1,2,0:T(8,128)}, f32[192,768]{1,0:T(8,128)}, f32[768,768]{1,0:T(8,128)}, ...) | async-done | bytes 7864336 | tf_op jit(solution)/shard_map/psum | solution.py:300
  1115.0 91.4 %reduce-scatter.2.cloned.1.call-done = f32[1024,128]{1,0:T(8,128)} async-done(((f32[8192,128]{1,0:T(8,128)}), f32[1024,128]{1,0:T(8,128)}) %reduce-scatter.2.cloned.1.call-update) | async-done | bytes 524304 | tf_op jit(solution)/shard_map/reduce_scatter | solution.py:296
  (620 shorter events, 326.1 us)
Async XLA Ops:
  7.2 315.8 %copy-start = (bf16[768,768]{1,0:T(8,128)(2,1)S(1)}, bf16[768,768]{1,0:T(8,128)(2,1)}, u32[]{:S(2)}) copy-start(bf16[768,768]{1,0:T(8,128)(2,1)} %param.45) | copy-start | bytes 3538948
  7.2 54.8 %all-gather.4.cloned.1.call-start = ((), (), s32[]{:S(2)}) async-start(), calls=%async_computation.1 | async-start | bytes 2359296 | tf_op jit(solution)/shard_map/all_gather | solution.py:214
  7.9 305.9 %all-reduce.7.cloned.1.call-start = ((), (), s32[]{:S(2)}) async-start(), calls=%async_computation.2 | async-start | bytes 12582912 | tf_op jit(solution)/shard_map/psum | solution.py:242
  9.4 68.8 %copy-start.51 = (pred[2048]{0:T(1024)(128)(4,1)}, pred[2048]{0:T(1024)(128)(4,1)S(1)}, u32[]{:S(2)}) copy-start(pred[2048]{0:T(1024)(128)(4,1)S(1)} %compare_and_fusion) | copy-start | bytes 6148
  11.4 66.8 %copy-start.39 = (f32[2048]{0:T(1024)}, f32[2048]{0:T(1024)S(1)}, u32[]{:S(2)}) copy-start(f32[2048]{0:T(1024)S(1)} %get-tuple-element.1363) | copy-start | bytes 24580
  13.5 69.2 %copy-start.23 = (bf16[2048,64]{0,1:T(8,128)(2,1)}, bf16[2048,64]{0,1:T(8,128)(2,1)S(1)}, u32[]{:S(2)}) copy-start(bf16[2048,64]{0,1:T(8,128)(2,1)S(1)} %get-tuple-element.1359) | copy-start | bytes 786436
  13.5 69.2 %copy-start.25 = (bf16[2048,64]{0,1:T(8,128)(2,1)}, bf16[2048,64]{0,1:T(8,128)(2,1)S(1)}, u32[]{:S(2)}) copy-start(bf16[2048,64]{0,1:T(8,128)(2,1)S(1)} %get-tuple-element.1360) | copy-start | bytes 786436
  70.5 11.1 copy-start.35
  90.6 101.3 %copy-start.29 = (bf16[192,768]{1,0:T(8,128)(2,1)S(1)}, bf16[192,768]{1,0:T(8,128)(2,1)}, u32[]{:S(2)}) copy-start(bf16[192,768]{1,0:T(8,128)(2,1)} %param.42) | copy-start | bytes 884740
  188.8 6.8 copy-start.7
  195.6 315.7 %all-gather.6.cloned.1.call-start = ((), (), s32[]{:S(2)}) async-start(), calls=%async_computation.4 | async-start | bytes 31457280 | tf_op jit(solution)/shard_map/all_gather | solution.py:211
  320.9 20.9 %slice-start.2 = ((s8[6291456]{0:T(1024)(128)(4,1)}), s8[4194304]{0:T(1024)(128)(4,1)S(1)}, s32[]{:S(2)}) async-start(s8[6291456]{0:T(1024)(128)(4,1)} %bitcast.206), calls=%async_computation.9 | async-start | bytes 8388608
  322.9 18.8 %copy-start.21 = (bf16[2048,768]{0,1:T(8,128)(2,1)}, bf16[2048,768]{0,1:T(8,128)(2,1)S(1)}, u32[]{:S(2)}) copy-start(bf16[2048,768]{0,1:T(8,128)(2,1)S(1)} %add_convert_fusion.2) | copy-start | bytes 9437188
  323.0 18.8 %slice-start.3 = ((s8[6291456]{0:T(1024)(128)(4,1)}), s8[2097152]{0:T(1024)(128)(4,1)S(1)}, s32[]{:S(2)}) async-start(s8[6291456]{0:T(1024)(128)(4,1)} %bitcast.206), calls=%async_computation.10 | async-start | bytes 4194304
  323.0 18.8 %copy-start.60 = (bf16[768,768]{1,0:T(8,128)(2,1)S(1)}, bf16[768,768]{1,0:T(8,128)(2,1)}, u32[]{:S(2)}) copy-start(bf16[768,768]{1,0:T(8,128)(2,1)} %param.47) | copy-start | bytes 3538948
  356.1 481.2 %all-reduce.11.cloned.1.call-start = ((), (), s32[]{:S(2)}) async-start(), calls=%async_computation.6 | async-start | bytes 12582912 | tf_op jit(solution)/shard_map/psum | solution.py:249
  530.6 6.4 copy-start.6
  530.6 10.6 slice-start.4
  709.1 8.5 copy-start.31
  717.6 397.4 %all-reduce.9.cloned.1.call-start = ((), (), s32[]{:S(2)}) async-start(), calls=%async_computation.5 | async-start | bytes 15728640 | tf_op jit(solution)/shard_map/psum | solution.py:300
  717.9 7.0 copy-start.22
  724.9 7.1 copy-start.9
  724.9 7.1 copy-start.15
  724.9 9.1 copy-start.20
  724.9 9.1 copy-start.30
  724.9 9.1 copy-start.32
  724.9 9.1 copy-start.34
  734.0 103.4 %copy-start.38 = (f32[2048]{0:T(1024)S(1)}, f32[2048]{0:T(1024)}, u32[]{:S(2)}) copy-start(f32[2048]{0:T(1024)} %copy-done.37) | copy-start | bytes 24580
  734.0 103.4 %copy-start.50 = (f32[768]{0:T(1024)S(1)}, f32[768]{0:T(1024)}, u32[]{:S(2)}) copy-start(f32[768]{0:T(1024)} %param.39) | copy-start | bytes 9220
  734.0 114.9 %slice-start.6 = ((s8[6291456]{0:T(1024)(128)(4,1)}), s8[2097152]{0:T(1024)(128)(4,1)S(1)}, s32[]{:S(2)}) async-start(s8[6291456]{0:T(1024)(128)(4,1)} %bitcast.210), calls=%async_computation.13 | async-start | bytes 4194304
  737.3 105.9 %copy-start.48 = (f32[2048]{0:T(1024)S(1)}, f32[2048]{0:T(1024)}, u32[]{:S(2)}) copy-start(f32[2048]{0:T(1024)} %copy-done.47) | copy-start | bytes 24580
  737.3 105.9 %copy-start.44 = (f32[2048]{0:T(1024)S(1)}, f32[2048]{0:T(1024)}, u32[]{:S(2)}) copy-start(f32[2048]{0:T(1024)} %copy-done.43) | copy-start | bytes 24580
  837.4 5.8 copy-start.10
  837.4 11.6 slice-start
  837.4 11.6 slice-start.7
  843.1 5.8 copy-start.46
  849.0 5.8 copy-start.24
  849.0 5.8 copy-start.26
  849.0 7.8 copy-start.17
  858.8 19.6 %copy-start.11 = (bf16[8192,128]{1,0:T(8,128)(2,1)S(1)}, bf16[8192,128]{1,0:T(8,128)(2,1)}, u32[]{:S(2)}) copy-start(bf16[8192,128]{1,0:T(8,128)(2,1)} %all-gather.4.cloned.1.call-done) | copy-start | bytes 6291460
  858.8 19.6 %copy-start.42 = (f32[8192]{0:T(1024)S(1)}, f32[8192]{0:T(1024)}, u32[]{:S(2)}) copy-start(f32[8192]{0:T(1024)} %get-tuple-element.1357) | copy-start | bytes 98308
  858.8 347.6 %reduce-scatter.2.cloned.1.call-start = ((), (), s32[]{:S(2)}) async-start(), calls=%async_computation.3 | async-start | bytes 4718592 | tf_op jit(solution)/shard_map/reduce_scatter | solution.py:296
  888.6 11.8 copy-start.58
  907.8 7.0 copy-start.54
  907.8 7.0 copy-start.59
  1114.9 101.3 %copy-start.27 = (f32[768,768]{1,0:T(8,128)S(1)}, f32[768,768]{1,0:T(8,128)}, u32[]{:S(2)}) copy-start(f32[768,768]{1,0:T(8,128)} %get-tuple-element.2152) | copy-start | bytes 7077892
  1206.3 8.5 copy-start.28
  1208.2 9.4 copy-start.1
  (30 other events, 64.1 us)
Sparse Core Ops, SparseCore 0:
  10.1 51.7 all-gather.3
  195.7 118.1 all-reduce.6
  356.2 154.9 all-gather.5
  717.7 119.6 all-reduce.10
  858.9 256.0 all-reduce.8
  1119.0 87.2 reduce-scatter.1
